TPU v7x, 256 devices: a whole 4x4x8 slice. The times are simulated.
256 devices in a mesh: head: 4 (over x), page: 64 (over y, z, core).
Axes of the slice: x: 4, y: 4, z: 8, core: 2. Of those that a mesh axis runs over, the one named last changes fastest.
Arguments:
- hidden: bfloat16 [12, 2048], P(None, 'page'), may hold values from -6 to 6
- q_weight: bfloat16 [2048, 3072], P('page', 'head'), may hold values from -0.125 to 0.125
- key_up: bfloat16 [16, 128, 512], P('head'), may hold values from -0.5 to 0.5
- value_up_weight: bfloat16 [16, 512, 128], P('head'), may hold values from -0.25 to 0.25
- out_weight: bfloat16 [2048, 2048], P('head', 'page'), may hold values from -0.125 to 0.125
- cache: bfloat16 [16, 512, 128, 576], P('head', 'page'), may hold values from -360 to 360
- page_table: int32 [16, 512], P('head', 'page'), may hold values from 0 to 511, each once within a row
- seq_pages: int32 [12], replicated, may hold values from 1 to 128, 512 in all
- keep_rows: int32 [16, 512, 64], P('head'), may hold values from 0 to 127, as said below
- fold_mass: bfloat16 [16, 512, 64], P('head'), may hold values from 0.5 to 4
- new_place: int32 [16, 512], P('head'), may hold values from 0 to 2047, as said below
- norm_gain: bfloat16 [2048], replicated, may hold values from 0.099609375 to 1.8984375
- router: bfloat16 [2048, 64], replicated, may hold values from -0.125 to 0.125
- routes: int32 [12, 6], replicated, may hold values from 0 to 63, all different within a row
- w_gate: bfloat16 [64, 2048, 1408], P('page', None, 'head'), may hold values from -0.125 to 0.125
- w_up: bfloat16 [64, 2048, 1408], P('page', None, 'head'), may hold values from -0.125 to 0.125
- w_down: bfloat16 [64, 1408, 2048], P('page', 'head'), may hold values from -0.15625 to 0.15625
Outputs:
- attn_out: bfloat16 [12, 2048], replicated
- moe_out: bfloat16 [12, 2048], replicated
- new_rows: bfloat16 [8192, 64, 576], P(('head', 'page'))
- new_mass: bfloat16 [8192, 64], P(('head', 'page'))
Inputs may be any that keep to these rules, and one draw needn't show every extreme that they name: `keep_rows`: the 64 entries of each head and page are distinct. `new_place`: for each group of heads h // 4 the places form a permutation of 0 to 2047. Among the blocks of one head group whose pages share g // 8, at most 1 have places with the same place // 32, and some reach 1.
All inputs are finite; a program needn't handle non-finite values.
Results may differ from a plain program's by a relative error of at most 0.035.
Values may be sent and summed in bfloat16 or wider, within the bound.
A program may use at most 128 MiB of HBM per device.

v0:
```python
import jax
import jax.numpy as jnp
from jax import lax
from jax.sharding import PartitionSpec as P

QK_NOPE = 128
QK_ROPE = 64
THETA = 50000.0
ROUTE_SCALE = 2.446
NORM_EPS = 1e-06


def joined_2(part, axis, combine):
    gathered = jax.tree.map(lambda a: lax.all_gather(a, axis), part)

    def take(source):
        return jax.tree.map(lambda a: lax.dynamic_index_in_dim(a, source, 0, False), gathered)

    return lax.fori_loop(
        1, lax.axis_size(axis), lambda source, state: combine(state, take(source)), take(0)
    )


def rotate_query(values, positions):
    half_dim = values.shape[-1] // 2
    freqs = THETA ** (-2.0 * jnp.arange(half_dim, dtype=jnp.float32) / values.shape[-1])
    angles = positions.astype(jnp.float32)[:, None] * freqs[None, :]
    cosine = jnp.cos(angles)[:, None, :]
    sine_v = jnp.sin(angles)[:, None, :]
    front = values[..., :half_dim]
    back = values[..., half_dim:]
    return jnp.concatenate(
        [front * cosine - back * sine_v, back * cosine + front * sine_v], axis=-1
    )


def pick_rows(one_page, row_ids):
    return one_page[row_ids]


def merge_parts(left_part, right_part):
    joined = jnp.maximum(left_part[0], right_part[0])
    left_factor = jnp.exp(left_part[0] - joined)
    right_factor = jnp.exp(right_part[0] - joined)
    return (
        joined,
        left_part[1] * left_factor + right_part[1] * right_factor,
        left_part[2] * left_factor[..., None] + right_part[2] * right_factor[..., None],
    )


def shards(
    hidden,
    q_weight,
    key_up,
    value_up_weight,
    out_weight,
    cache,
    page_table,
    seq_pages,
    keep_rows,
    fold_mass,
    new_place,
    norm_gain,
    router,
    routes,
    w_gate,
    w_up,
    w_down,
):
    heads_here = key_up.shape[0]
    pages_here = cache.shape[1]
    page_rows = cache.shape[2]
    latent_dim = cache.shape[3]
    kv_rank = key_up.shape[2]
    kept_count = keep_rows.shape[2]
    requests = hidden.shape[0]
    head_size = QK_NOPE + QK_ROPE
    groups = lax.axis_size("page")
    page_index = lax.axis_index("page")
    blocks = heads_here * pages_here
    sending_limit = (blocks + groups - 1) // groups
    first_page = page_index * pages_here
    partial_value = jnp.dot(hidden, q_weight, preferred_element_type=jnp.float32)
    queries = lax.psum(partial_value, "page").reshape(requests, heads_here, head_size)
    q_nope = queries[..., :QK_NOPE].astype(jnp.bfloat16)
    positions = seq_pages * page_rows - 1
    q_rope = rotate_query(queries[..., QK_NOPE:], positions).astype(jnp.bfloat16)
    q_latent = jnp.einsum(
        "rhn,hnk->rhk", q_nope, key_up, preferred_element_type=jnp.float32
    ).astype(jnp.bfloat16)
    q_full = jnp.concatenate([q_latent, q_rope], axis=-1)
    keep_here = lax.dynamic_slice_in_dim(keep_rows, first_page, pages_here, 1)
    mass_here = lax.dynamic_slice_in_dim(fold_mass, first_page, pages_here, 1)
    compact = jax.vmap(jax.vmap(pick_rows))(cache, keep_here)
    flat_rows = compact.reshape(heads_here, pages_here * kept_count, latent_dim)
    page_ends = jnp.cumsum(seq_pages)
    owner = jnp.sum((page_table[..., None] >= page_ends).astype(jnp.int32), axis=-1)
    row_owner = jnp.repeat(owner, kept_count, axis=1)
    in_request = row_owner[:, None, :] == jnp.arange(requests, dtype=jnp.int32)[None, :, None]
    scores = jnp.einsum(
        "rhk,hnk->hrn", q_full, flat_rows, preferred_element_type=jnp.float32
    ) * head_size ** (-0.5)
    row_max = jnp.max(jnp.where(in_request, scores, -1e30), axis=-1)
    row_mass = mass_here.reshape(heads_here, 1, pages_here * kept_count).astype(jnp.float32)
    weights = jnp.where(in_request, row_mass * jnp.exp(scores - row_max[..., None]), 0.0)
    totals = jnp.sum(weights, axis=-1)
    weighted = jnp.einsum(
        "hrn,hnk->hrk",
        weights.astype(jnp.bfloat16),
        flat_rows[..., :kv_rank],
        preferred_element_type=jnp.float32,
    )
    best, mass_sum, latent_sum = joined_2((row_max, totals, weighted), "page", merge_parts)
    latent_output = (latent_sum / mass_sum[..., None]).astype(jnp.bfloat16)
    head_result_rows = jnp.einsum(
        "usj,ujb->sub", latent_output, value_up_weight, preferred_element_type=jnp.float32
    ).astype(jnp.bfloat16)
    head_result_rows = head_result_rows.reshape(requests, heads_here * value_up_weight.shape[2])
    out_cols = jnp.dot(head_result_rows, out_weight, preferred_element_type=jnp.float32)
    col_width = out_cols.shape[1]
    padded = jnp.zeros((requests, col_width * groups), jnp.float32)
    padded = lax.dynamic_update_slice_in_dim(padded, out_cols, page_index * col_width, 1)
    attn_out = lax.psum(padded, ("head", "page")).astype(jnp.bfloat16)
    attn_wide = attn_out.astype(jnp.float32)
    mean_sq = jnp.mean(attn_wide * attn_wide, axis=-1, keepdims=True)
    normed = (attn_wide * lax.rsqrt(mean_sq + NORM_EPS) * norm_gain.astype(jnp.float32)).astype(
        jnp.bfloat16
    )
    logits = jnp.dot(normed, router, preferred_element_type=jnp.float32)
    picked = jax.nn.sigmoid(jnp.take_along_axis(logits, routes, axis=1))
    shares = ROUTE_SCALE * picked / jnp.sum(picked, axis=1, keepdims=True)
    expert_ids = jnp.arange(logits.shape[1], dtype=jnp.int32)
    combine = jnp.sum(
        jnp.where(routes[:, :, None] == expert_ids[None, None, :], shares[:, :, None], 0.0), axis=1
    )
    local_experts = w_gate.shape[0]
    combine_here = lax.dynamic_slice_in_dim(combine, page_index * local_experts, local_experts, 1)
    gate_part = jnp.einsum("rd,edf->erf", normed, w_gate, preferred_element_type=jnp.float32)
    up_part = jnp.einsum("rd,edf->erf", normed, w_up, preferred_element_type=jnp.float32)
    expert_hidden = (jax.nn.silu(gate_part) * up_part).astype(jnp.bfloat16)
    expert_outs = jnp.einsum(
        "erf,efd->erd", expert_hidden, w_down, preferred_element_type=jnp.float32
    )
    expert_terms = jnp.sum(combine_here.T[:, :, None] * expert_outs, axis=0)
    moe_out = lax.psum(expert_terms, ("head", "page")).astype(jnp.bfloat16)
    dest_all = new_place // blocks
    slot_all = new_place % blocks
    dest_here = lax.dynamic_slice_in_dim(dest_all, first_page, pages_here, 1).reshape(blocks)
    peer_ids = jnp.arange(groups, dtype=jnp.int32)
    dest_onehot = (dest_here[:, None] == peer_ids[None, :]).astype(jnp.int32)
    send_rank = jnp.sum(jnp.cumsum(dest_onehot, axis=0) * dest_onehot, axis=1) - 1
    send_col = dest_here * sending_limit + send_rank
    slot_ids = jnp.arange(groups * sending_limit, dtype=jnp.int32)
    chooser = (send_col[:, None] == slot_ids[None, :]).astype(jnp.bfloat16)

    def arrange(values):
        return (
            values.reshape(heads_here, groups, pages_here)
            .transpose(1, 0, 2)
            .reshape(groups, blocks)
        )

    to_here = arrange(dest_all) == page_index
    recv_rank = jnp.cumsum(to_here.astype(jnp.int32), axis=1) - 1
    recv_col = peer_ids[:, None] * sending_limit + recv_rank
    block_ids = jnp.arange(blocks, dtype=jnp.int32)
    by_slot = ((arrange(slot_all)[..., None] == block_ids) & to_here[..., None]).astype(
        jnp.bfloat16
    )
    by_col = (recv_col[..., None] == slot_ids).astype(jnp.bfloat16)
    unpack = jnp.einsum("sbq,sbc->qc", by_slot, by_col, preferred_element_type=jnp.float32).astype(
        jnp.bfloat16
    )
    owned = (slot_all.reshape(-1)[None, :] == block_ids[:, None]) & (
        dest_all.reshape(-1)[None, :] == page_index
    )
    new_mass = jnp.dot(
        owned.astype(jnp.bfloat16),
        fold_mass.reshape(-1, kept_count),
        preferred_element_type=jnp.float32,
    ).astype(jnp.bfloat16)
    payload = cache.reshape(blocks, page_rows * latent_dim)
    outgoing = jnp.einsum("bc,bx->cx", chooser, payload, preferred_element_type=jnp.float32).astype(
        jnp.bfloat16
    )
    arrived_rows = lax.all_to_all(
        outgoing.reshape(groups, sending_limit, page_rows, latent_dim),
        "page",
        split_axis=0,
        concat_axis=0,
        tiled=True,
    )
    placed = jnp.dot(
        unpack,
        arrived_rows.reshape(groups * sending_limit, page_rows * latent_dim),
        preferred_element_type=jnp.float32,
    ).astype(jnp.bfloat16)
    keep_new = jnp.dot(owned.astype(jnp.int32), keep_rows.reshape(-1, kept_count))
    new_rows = jax.vmap(pick_rows)(placed.reshape(blocks, page_rows, latent_dim), keep_new)
    return (attn_out, moe_out, new_rows, new_mass)


def solution(mesh):
    in_specs = (
        P(None, "page"),
        P("page", "head"),
        P("head", None, None),
        P("head", None, None),
        P("head", "page"),
        P("head", "page", None, None),
        P("head", "page"),
        P(),
        P("head", None, None),
        P("head", None, None),
        P("head", None),
        P(),
        P(),
        P(),
        P("page", None, "head"),
        P("page", None, "head"),
        P("page", "head", None),
    )
    out_specs = (P(), P(), P(("head", "page"), None, None), P(("head", "page"), None))
    return jax.shard_map(shards, mesh=mesh, in_specs=in_specs, out_specs=out_specs, check_vma=False)
```

profile of v0, /device:TPU:1, one launch (start us, length us, event | category | flops | bytes accessed | tf_op | source)
XLA Modules:
  0.0 994.9 jit_solution(4305672104055780673)
XLA Ops:
  7.3 1.1 constant_dynamic-slice_fusion.2
  8.6 7.8 copy.109
  16.6 249.7 %psum.21 = f32[12,4,192]{2,0,1:T(8,128)S(1)} all-reduce(f32[12,4,192]{2,0,1:T(8,128)S(1)} %copy.107), channel_id=1, replica_groups=mesh['head'=4,'page'=64] {'page'}, use_global_device_ids=true, to_apply=%region_2.3 | all-reduce | flops 9216 | bytes 73728 | tf_op jit(solution)/shard_map/psum | solution.py:85
  267.1 39.7 %gather_fusion = bf16[2048,576]{1,0:T(8,128)(2,1)} fusion(bf16[4,8,128,576]{3,2,1,0:T(8,128)(2,1)} %copy.109, s32[2048]{0:T(1024)S(1)} %reshape.256), kind=kCustom, calls=%fused_computation | custom fusion | bytes 4743168 | tf_op jit(solution)/shard_map/vmap(vmap())/gather | solution.py:38
  307.2 2.8 select_reduce_fusion
  310.0 1.1 fusion.3
  311.2 8.8 reshape.249
  320.5 8.7 convolution_convert_fusion
  329.2 15.5 %reshape.250 = bf16[64,1,128,576]{3,2,0,1:T(8,128)(2,1)} reshape(bf16[64,73728]{1,0:T(8,128)(2,1)} %convolution_convert_fusion) | data formatting | bytes 18874368 | tf_op jit(solution)/shard_map/reshape | solution.py:188
  344.7 13.9 %copy.123 = bf16[64,1,128,576]{2,3,1,0:T(8,128)(2,1)} copy(bf16[64,1,128,576]{3,2,0,1:T(8,128)(2,1)} %reshape.250) | data formatting | bytes 18874368 | tf_op jit(solution)/shard_map/reshape | solution.py:188
  358.6 10.9 %all-to-all-start = ((bf16[64,1,128,576]{2,3,1,0:T(8,128)(2,1)}), bf16[64,1,128,576]{2,3,1,0:T(8,128)(2,1)}, u32[]{:S(2)}, u32[]{:S(2)}) async-start(bf16[64,1,128,576]{2,3,1,0:T(8,128)(2,1)} %copy.123), calls=%async_computation | async-start | bytes 18874368 | tf_op jit(solution)/shard_map/all_to_all | solution.py:187
  371.6 259.4 %all-gather.4 = f32[64,4,12]{2,1,0:T(4,128)S(1)} all-gather(f32[1,4,12]{2,1,0:T(4,128)S(1)} %bitcast.156), channel_id=3, replica_groups=mesh['head'=4,'page'=64] {'page'}, dimensions={0}, use_global_device_ids=true | all-gather | bytes 12480 | tf_op jit(solution)/shard_map/all_gather | solution.py:14
  631.0 47.8 %all-gather.3 = f32[64,4,12]{2,1,0:T(4,128)S(1)} all-gather(f32[1,4,12]{2,1,0:T(4,128)S(1)} %bitcast.154), channel_id=2, replica_groups=mesh['head'=4,'page'=64] {'page'}, dimensions={0}, use_global_device_ids=true | all-gather | bytes 12480 | tf_op jit(solution)/shard_map/all_gather | solution.py:14
  680.5 66.4 %while.19 = (s32[]{:T(128)}, f32[4,12]{1,0:T(4,128)S(1)}, f32[4,12]{1,0:T(4,128)S(1)}, f32[4,12,512]{2,1,0:T(8,128)S(1)}, f32[64,4,12]{2,1,0:T(4,128)S(1)}, /*in...) while((s32[]{:T(128)}, f32[4,12]{1,0:T(4,128)S(1)}, ...), condition=%wide.region_6.7_spmd, body=%wide.region_5.6_spmd.sunk | while | flops 74021 | bytes 296983 | solution.py:19
  746.9 1.3 fusion.23
  748.8 75.9 %psum.22 = bf16[12,2048]{1,0:T(8,128)(2,1)S(1)} all-reduce(f32[12,2048]{1,0:T(8,128)S(1)} %dynamic_update_slice.3), channel_id=1, replica_groups=mesh['head'=4,'page'=64] {'head','page'}, use_global_device_ids=true, to_apply=%region_7.8 | all-reduce | flops 24576 | bytes 147456 | tf_op jit(solution)/shard_map/psum | solution.py:124
  825.1 1.7 gather_fusion.1
  827.9 2.5 convolution_multiply_fusion
  830.4 73.9 %psum.23 = bf16[12,2048]{1,0:T(8,128)(2,1)} all-reduce(f32[12,2048]{1,0:T(8,128)S(1)} %convolution_multiply_fusion), channel_id=1, replica_groups=mesh['head'=4,'page'=64] {'head','page'}, use_global_device_ids=true, to_apply=%region_11.12 | all-reduce | flops 24576 | bytes 147456 | tf_op jit(solution)/shard_map/psum | solution.py:146
  904.3 14.1 %copy.124 = bf16[64,1,128,576]{3,2,0,1:T(8,128)(2,1)} copy(bf16[64,1,128,576]{2,3,1,0:T(8,128)(2,1)} %all-to-all-done) | data formatting | bytes 18874368 | tf_op jit(solution)/shard_map/all_to_all | solution.py:187
  918.4 15.3 %reshape.251 = bf16[64,73728]{1,0:T(8,128)(2,1)} reshape(bf16[64,1,128,576]{3,2,0,1:T(8,128)(2,1)} %copy.124) | data formatting | bytes 18874368 | tf_op jit(solution)/shard_map/reshape | solution.py:196
  933.6 8.0 convolution_convert_fusion.1
  941.7 8.8 reshape.252
  950.5 37.5 %gather_fusion.2 = bf16[2048,576]{1,0:T(8,128)(2,1)} fusion(bf16[32,128,576]{2,1,0:T(8,128)(2,1)} %reshape.252, s32[2048]{0:T(1024)S(1)} %reshape.268), kind=kCustom, calls=%fused_computation.2 | custom fusion | bytes 4734976 | tf_op jit(solution)/shard_map/vmap()/gather | solution.py:38
  (232 shorter events, 72.5 us)
Async XLA Ops:
  7.2 820.7 %copy-start = (bf16[1,352,2048]{2,1,0:T(8,128)(2,1)S(1)}, bf16[1,352,2048]{2,1,0:T(8,128)(2,1)}, u32[]{:S(2)}) copy-start(bf16[1,352,2048]{2,1,0:T(8,128)(2,1)} %param.35) | copy-start | bytes 4325380
  7.2 672.4 %all-gather.7.cloned.1.call-start = ((), (), s32[]{:S(2)}) async-start(), calls=%async_computation.1 | async-start | bytes 8519680 | tf_op jit(solution)/shard_map/all_gather | solution.py:14
  8.5 7.8 copy-start.8
  8.5 7.8 copy-start.11
  8.5 257.7 %copy-start.15 = (s32[12]{0:T(128)S(1)}, s32[12]{0:T(128)}, u32[]{:S(2)}) copy-start(s32[12]{0:T(128)} %param.26) | copy-start | bytes 148
  8.5 257.9 %copy-start.13 = (s32[4,8]{1,0:T(4,128)S(1)}, s32[4,8]{1,0:T(4,128)}, u32[]{:S(2)}) copy-start(s32[4,8]{1,0:T(4,128)} %param.25) | copy-start | bytes 388
  8.5 258.3 %copy-start.6 = (bf16[4,512,64]{1,2,0:T(8,128)(2,1)S(1)}, bf16[4,512,64]{1,2,0:T(8,128)(2,1)}, u32[]{:S(2)}) copy-start(bf16[4,512,64]{1,2,0:T(8,128)(2,1)} %param.28) | copy-start | bytes 786436
  267.1 39.8 %copy-start.5 = (bf16[4,128,512]{2,1,0:T(8,128)(2,1)S(1)}, bf16[4,128,512]{2,1,0:T(8,128)(2,1)}, u32[]{:S(2)}) copy-start(bf16[4,128,512]{2,1,0:T(8,128)(2,1)} %param.21) | copy-start | bytes 1572868
  306.8 3.2 copy-start.1
  311.2 8.8 copy-start.7
  358.6 10.9 %copy-start.12 = (bf16[2048]{0:T(1024)(128)(2,1)S(1)}, bf16[2048]{0:T(1024)(128)(2,1)}, u32[]{:S(2)}) copy-start(bf16[2048]{0:T(1024)(128)(2,1)} %param.30) | copy-start | bytes 12292
  358.6 10.9 %copy-start.9 = (s32[12,6]{0,1:T(8,128)S(1)}, s32[12,6]{0,1:T(8,128)}, u32[]{:S(2)}) copy-start(s32[12,6]{0,1:T(8,128)} %param.32) | copy-start | bytes 868
  358.6 12.2 %copy-start.4 = (s32[4,512,64]{1,2,0:T(8,128)S(1)}, s32[4,512,64]{1,2,0:T(8,128)}, u32[]{:S(2)}) copy-start(s32[4,512,64]{1,2,0:T(8,128)} %param.27) | copy-start | bytes 1572868
  358.6 545.7 %all-to-all-start = ((bf16[64,1,128,576]{2,3,1,0:T(8,128)(2,1)}), bf16[64,1,128,576]{2,3,1,0:T(8,128)(2,1)}, u32[]{:S(2)}, u32[]{:S(2)}) async-start(bf16[64,1,128,576]{2,3,1,0:T(8,128)(2,1)} %copy.123), calls=%async_computation | async-start | bytes 18874368 | tf_op jit(solution)/shard_map/all_to_all | solution.py:187
  370.8 377.4 %copy-start.10 = (bf16[512,32]{0,1:T(8,128)(2,1)S(1)}, bf16[512,32]{0,1:T(8,128)(2,1)}, u32[]{:S(2)}) copy-start(bf16[512,32]{0,1:T(8,128)(2,1)} %param.23) | copy-start | bytes 98308
  371.4 453.5 %copy-start.14 = (bf16[2048,64]{0,1:T(8,128)(2,1)S(1)}, bf16[2048,64]{0,1:T(8,128)(2,1)}, u32[]{:S(2)}) copy-start(bf16[2048,64]{0,1:T(8,128)(2,1)} %param.31) | copy-start | bytes 786436
  824.7 3.2 copy-start.3
  825.1 2.3 copy-start.2
Sparse Core Ops, SparseCore 0:
  311.3 121.7 all-gather.6
where the time goes:
time: 999 us; the launch traced here: 995 us
  blocking collectives  707 us (71%)
  local copies, waits for them, and re-layouts  168 us (17%)
  other arithmetic  66.3 us (7%)
  matrix products  26.8 us (3%)
  between operations  14.4 us (1%)
  starting transfers between devices  10.9 us (1%)
    all_gather x2, blocking collectives, joined_2(): gathered = jax.tree.map(lambda a: lax.all_gather(a, axis), part)  307 us
    psum x1, blocking collectives, shards(): lax.psum(partial_value, 'page').reshape(requests, heads_here, head_size)  250 us
    gather x4, local copies, waits for them, and re-layouts, pick_rows(): return one_page[row_ids]  77.4 us
    psum x1, blocking collectives, shards(): attn_out = lax.psum(padded, ('head', 'page')).astype(jnp.bfloat16)  75.9 us
    psum x1, blocking collectives, shards(): moe_out = lax.psum(expert_terms, ('head', 'page')).astype(jnp.bfloat16)  73.9 us
    add x63, other arithmetic, merge_parts(): left_part[2] * left_factor[..., None]  62.9 us
    reshape x2, local copies, waits for them, and re-layouts, shards(): outgoing.reshape(groups, sending_limit, page_rows, latent_dim)  29.4 us
  transfers between devices with their start and end apart: 2, of which 0 were waited for; matrix products, arithmetic and copies ran while one was open for 12% of the time, Pallas kernels for 0%

commit v1 on v0

--- a/solution.py
+++ b/solution.py
@@ -121,7 +121,7 @@
     col_width = out_cols.shape[1]
     padded = jnp.zeros((requests, col_width * groups), jnp.float32)
     padded = lax.dynamic_update_slice_in_dim(padded, out_cols, page_index * col_width, 1)
-    attn_out = lax.psum(padded, ("head", "page")).astype(jnp.bfloat16)
+    attn_out = lax.psum(lax.psum(padded, "page"), "head").astype(jnp.bfloat16)
     attn_wide = attn_out.astype(jnp.float32)
     mean_sq = jnp.mean(attn_wide * attn_wide, axis=-1, keepdims=True)
     normed = (attn_wide * lax.rsqrt(mean_sq + NORM_EPS) * norm_gain.astype(jnp.float32)).astype(

time: 999 us -> 1110 us (1.11)
  waiting for transfers between devices: 0.02 us -> 171 us
  blocking collectives: 707 us -> 649 us
    psum x0 -> x1, waiting for transfers between devices: none -> 171 us  [shards(): attn_out = lax.psum(lax.psum(padded, 'page'), 'head').astype(jnp.bfloat16)]
    psum x1, blocking collectives: 75.9 us -> 15 us  [shards(): attn_out = lax.psum(lax.psum(padded, 'page'), 'head').astype(jnp.bfloat16)]
  transfers between devices with their start and end apart: 2 -> 3, of which waited for: 0 -> 1; matrix products, arithmetic and copies ran while one was open for 12% -> 11% of each run, Pallas kernels for 0% -> 0%
where the time goes in v1:
time: 1110 us
  blocking collectives  649 us (58%)
  waiting for transfers between devices  171 us (15%)
  local copies, waits for them, and re-layouts  169 us (15%)
  other arithmetic  66.2 us (6%)
  matrix products  26.8 us (2%)
  between operations  14.4 us (1%)
    all_gather x2, blocking collectives, joined_2(): gathered = jax.tree.map(lambda a: lax.all_gather(a, axis), part)  308 us
    psum x1, blocking collectives, shards(): lax.psum(partial_value, 'page').reshape(requests, heads_here, head_size)  250 us
    psum x1, waiting for transfers between devices, shards(): attn_out = lax.psum(lax.psum(padded, 'page'), 'head').astype(jnp.bfloat16)  171 us
    gather x4, local copies, waits for them, and re-layouts, pick_rows(): return one_page[row_ids]  77.4 us
    psum x1, blocking collectives, shards(): moe_out = lax.psum(expert_terms, ('head', 'page')).astype(jnp.bfloat16)  76 us
    add x63, other arithmetic, merge_parts(): left_part[2] * left_factor[..., None]  62.9 us
    reshape x2, local copies, waits for them, and re-layouts, shards(): outgoing.reshape(groups, sending_limit, page_rows, latent_dim)  29.4 us
  transfers between devices with their start and end apart: 3, of which 1 were waited for; matrix products, arithmetic and copies ran while one was open for 11% of the time, Pallas kernels for 0%

profile of v1, /device:TPU:1, one launch (start us, length us, event | category | flops | bytes accessed | tf_op | source)
XLA Modules:
  0.0 1108.5 jit_solution(4651187013858797390)
XLA Ops:
  8.6 7.8 copy.109
  16.6 249.7 %psum.28 = f32[12,4,192]{2,0,1:T(8,128)S(1)} all-reduce(f32[12,4,192]{2,0,1:T(8,128)S(1)} %copy.107), channel_id=1, replica_groups=mesh['head'=4,'page'=64] {'page'}, use_global_device_ids=true, to_apply=%region_2.3 | all-reduce | flops 9216 | bytes 73728 | tf_op jit(solution)/shard_map/psum | solution.py:85
  267.1 39.7 %gather_fusion = bf16[2048,576]{1,0:T(8,128)(2,1)} fusion(bf16[4,8,128,576]{3,2,1,0:T(8,128)(2,1)} %copy.109, s32[2048]{0:T(1024)S(1)} %reshape.256), kind=kCustom, calls=%fused_computation | custom fusion | bytes 4743168 | tf_op jit(solution)/shard_map/vmap(vmap())/gather | solution.py:38
  307.2 2.8 select_reduce_fusion
  310.0 1.1 fusion.3
  311.2 8.8 reshape.249
  320.5 8.7 convolution_convert_fusion
  329.2 15.5 %reshape.250 = bf16[64,1,128,576]{3,2,0,1:T(8,128)(2,1)} reshape(bf16[64,73728]{1,0:T(8,128)(2,1)} %convolution_convert_fusion) | data formatting | bytes 18874368 | tf_op jit(solution)/shard_map/reshape | solution.py:188
  344.6 13.9 %copy.123 = bf16[64,1,128,576]{2,3,1,0:T(8,128)(2,1)} copy(bf16[64,1,128,576]{3,2,0,1:T(8,128)(2,1)} %reshape.250) | data formatting | bytes 18874368 | tf_op jit(solution)/shard_map/reshape | solution.py:188
  358.6 10.9 all-to-all-start
  370.4 260.6 %all-gather.4 = f32[64,4,12]{2,1,0:T(4,128)S(1)} all-gather(f32[1,4,12]{2,1,0:T(4,128)S(1)} %bitcast.156), channel_id=3, replica_groups=mesh['head'=4,'page'=64] {'page'}, dimensions={0}, use_global_device_ids=true | all-gather | bytes 12480 | tf_op jit(solution)/shard_map/all_gather | solution.py:14
  631.0 47.8 %all-gather.3 = f32[64,4,12]{2,1,0:T(4,128)S(1)} all-gather(f32[1,4,12]{2,1,0:T(4,128)S(1)} %bitcast.154), channel_id=2, replica_groups=mesh['head'=4,'page'=64] {'page'}, dimensions={0}, use_global_device_ids=true | all-gather | bytes 12480 | tf_op jit(solution)/shard_map/all_gather | solution.py:14
  681.0 66.3 %while.19 = (s32[]{:T(128)}, f32[4,12]{1,0:T(4,128)S(1)}, f32[4,12]{1,0:T(4,128)S(1)}, f32[4,12,512]{2,1,0:T(8,128)S(1)}, f32[64,4,12]{2,1,0:T(4,128)S(1)}, /*in...) while((s32[]{:T(128)}, f32[4,12]{1,0:T(4,128)S(1)}, ...), condition=%wide.region_6.7_spmd, body=%wide.region_5.6_spmd.sunk | while | flops 74021 | bytes 296983 | solution.py:19
  747.3 1.3 fusion.23
  750.5 170.7 %all-reduce.2.cloned.1.call-done = f32[12,2048]{1,0:T(8,128)} async-done(((f32[12,2048]{1,0:T(8,128)}), f32[12,2048]{1,0:T(8,128)}) %all-reduce.2.cloned.1.call-update) | async-done | bytes 98320 | tf_op jit(solution)/shard_map/psum | solution.py:124
  921.2 15.0 %psum.30 = bf16[12,2048]{1,0:T(8,128)(2,1)S(1)} all-reduce(f32[12,2048]{1,0:T(8,128)} %all-reduce.2.cloned.1.call-done), channel_id=1, replica_groups=mesh['head'=4,'page'=64] {'head'}, use_global_device_ids=true, to_apply=%region_8.9 | all-reduce | flops 24576 | bytes 147456 | tf_op jit(solution)/shard_map/psum | solution.py:124
  936.6 1.7 gather_fusion.1
  939.5 2.5 convolution_multiply_fusion
  942.0 76.0 %psum.31 = bf16[12,2048]{1,0:T(8,128)(2,1)} all-reduce(f32[12,2048]{1,0:T(8,128)S(1)} %convolution_multiply_fusion), channel_id=1, replica_groups=mesh['head'=4,'page'=64] {'head','page'}, use_global_device_ids=true, to_apply=%region_12.13 | all-reduce | flops 24576 | bytes 147456 | tf_op jit(solution)/shard_map/psum | solution.py:146
  1017.9 14.1 %copy.124 = bf16[64,1,128,576]{3,2,0,1:T(8,128)(2,1)} copy(bf16[64,1,128,576]{2,3,1,0:T(8,128)(2,1)} %all-to-all-done) | data formatting | bytes 18874368 | tf_op jit(solution)/shard_map/all_to_all | solution.py:187
  1032.0 15.3 %reshape.251 = bf16[64,73728]{1,0:T(8,128)(2,1)} reshape(bf16[64,1,128,576]{3,2,0,1:T(8,128)(2,1)} %copy.124) | data formatting | bytes 18874368 | tf_op jit(solution)/shard_map/reshape | solution.py:196
  1047.3 8.0 convolution_convert_fusion.1
  1055.3 8.8 reshape.252
  1064.1 37.5 %gather_fusion.2 = bf16[2048,576]{1,0:T(8,128)(2,1)} fusion(bf16[32,128,576]{2,1,0:T(8,128)(2,1)} %reshape.252, s32[2048]{0:T(1024)S(1)} %reshape.268), kind=kCustom, calls=%fused_computation.2 | custom fusion | bytes 4734976 | tf_op jit(solution)/shard_map/vmap()/gather | solution.py:38
  (237 shorter events, 74.2 us)
Async XLA Ops:
  7.2 932.3 %copy-start = (bf16[1,352,2048]{2,1,0:T(8,128)(2,1)S(1)}, bf16[1,352,2048]{2,1,0:T(8,128)(2,1)}, u32[]{:S(2)}) copy-start(bf16[1,352,2048]{2,1,0:T(8,128)(2,1)} %param.35) | copy-start | bytes 4325380
  7.2 672.9 %all-gather.7.cloned.1.call-start = ((), (), s32[]{:S(2)}) async-start(), calls=%async_computation.2 | async-start | bytes 8519680 | tf_op jit(solution)/shard_map/all_gather | solution.py:14
  8.5 7.8 copy-start.9
  8.5 7.8 copy-start.12
  8.5 257.7 %copy-start.16 = (s32[12]{0:T(128)S(1)}, s32[12]{0:T(128)}, u32[]{:S(2)}) copy-start(s32[12]{0:T(128)} %param.26) | copy-start | bytes 148
  8.5 257.9 %copy-start.14 = (s32[4,8]{1,0:T(4,128)S(1)}, s32[4,8]{1,0:T(4,128)}, u32[]{:S(2)}) copy-start(s32[4,8]{1,0:T(4,128)} %param.25) | copy-start | bytes 388
  8.5 258.3 %copy-start.7 = (bf16[4,512,64]{1,2,0:T(8,128)(2,1)S(1)}, bf16[4,512,64]{1,2,0:T(8,128)(2,1)}, u32[]{:S(2)}) copy-start(bf16[4,512,64]{1,2,0:T(8,128)(2,1)} %param.28) | copy-start | bytes 786436
  267.1 39.8 %copy-start.5 = (bf16[4,128,512]{2,1,0:T(8,128)(2,1)S(1)}, bf16[4,128,512]{2,1,0:T(8,128)(2,1)}, u32[]{:S(2)}) copy-start(bf16[4,128,512]{2,1,0:T(8,128)(2,1)} %param.21) | copy-start | bytes 1572868
  306.8 3.2 copy-start.1
  311.2 8.8 copy-start.8
  358.6 11.5 %copy-start.4 = (s32[4,512,64]{1,2,0:T(8,128)S(1)}, s32[4,512,64]{1,2,0:T(8,128)}, u32[]{:S(2)}) copy-start(s32[4,512,64]{1,2,0:T(8,128)} %param.27) | copy-start | bytes 1572868
  358.6 659.3 %all-to-all-start = ((bf16[64,1,128,576]{2,3,1,0:T(8,128)(2,1)}), bf16[64,1,128,576]{2,3,1,0:T(8,128)(2,1)}, u32[]{:S(2)}, u32[]{:S(2)}) async-start(bf16[64,1,128,576]{2,3,1,0:T(8,128)(2,1)} %copy.123), calls=%async_computation | async-start | bytes 18874368 | tf_op jit(solution)/shard_map/all_to_all | solution.py:187
  369.5 551.7 %all-reduce.2.cloned.1.call-start = ((), (), s32[]{:S(2)}) async-start(), calls=%async_computation.1 | async-start | bytes 262144 | tf_op jit(solution)/shard_map/psum | solution.py:124
  370.1 378.5 %copy-start.11 = (bf16[512,32]{0,1:T(8,128)(2,1)S(1)}, bf16[512,32]{0,1:T(8,128)(2,1)}, u32[]{:S(2)}) copy-start(bf16[512,32]{0,1:T(8,128)(2,1)} %param.23) | copy-start | bytes 98308
  370.2 379.6 %copy-start.10 = (s32[12,6]{0,1:T(8,128)S(1)}, s32[12,6]{0,1:T(8,128)}, u32[]{:S(2)}) copy-start(s32[12,6]{0,1:T(8,128)} %param.32) | copy-start | bytes 868
  370.2 379.7 %copy-start.13 = (bf16[2048]{0:T(1024)(128)(2,1)S(1)}, bf16[2048]{0:T(1024)(128)(2,1)}, u32[]{:S(2)}) copy-start(bf16[2048]{0:T(1024)(128)(2,1)} %param.30) | copy-start | bytes 12292
  678.8 257.6 %copy-start.15 = (bf16[2048,64]{0,1:T(8,128)(2,1)S(1)}, bf16[2048,64]{0,1:T(8,128)(2,1)}, u32[]{:S(2)}) copy-start(bf16[2048,64]{0,1:T(8,128)(2,1)} %param.31) | copy-start | bytes 786436
  749.1 0.7 copy-start.6
  936.2 3.2 copy-start.3
  936.6 2.3 copy-start.2
Sparse Core Ops, SparseCore 0:
  311.3 121.7 all-gather.6
  749.9 171.2 all-reduce.1
